TPU v7x, 256 devices: a whole 4x4x8 slice. The times are simulated.
256 devices in a mesh: tm: 32 (over z_lo, x, core), cells: 8 (over y, z_hi).
Axes of the slice: x: 4, y: 4, z: 8 (z_hi: 2, z_lo: 4; z = z_hi * 4 + z_lo), core: 2. Of those that a mesh axis runs over, the one named last changes fastest.
Arguments:
- hist_bin: int32 [16384, 8192], P('tm', 'cells'), may hold values from 0 to 255
- obs_bin: int32 [16384, 8192], P('tm', 'cells'), may hold values from 0 to 255
- fut_bin: int32 [16384, 8192], P('tm', 'cells'), may hold values from 0 to 255
- region_id: int32 [8192], P('cells'), may hold values from 0 to 127, as said below
- bin_width: float32 [8192], P('cells'), may hold values from 0.005 to 0.05
- bin_offset: float32 [8192], P('cells'), may hold values from -4 to 4
Outputs:
- adjusted: float32 [16384, 8192], P('tm', 'cells')
Inputs may be any that keep to these rules, and one draw needn't show every extreme that they name: `region_id`: every zone of 0 to 127 holds exactly 64 cells.
All inputs are finite; a program needn't handle non-finite values.
Results may differ from a plain program's by a relative error of at most 0.0003.
Values sent between devices are 32-bit elements; how exact they have to be, the bound alone decides.
A program may use at most 64 MiB of HBM per device.

v0:
```python
import math
import jax
import jax.numpy as jnp
from jax import lax
from jax.sharding import PartitionSpec as P

BINS = 256
REGIONS = 128
pool_weight = 0.5


def in_order(blocks, dim):
    blocks = jnp.moveaxis(blocks, 0, dim)
    dims = blocks.shape
    return blocks.reshape(*dims[:dim], dims[dim] * dims[dim + 1], *dims[dim + 2 :])


def copy_for_each(array, axis):
    count = lax.axis_size(axis)
    return lax.all_to_all(
        jnp.broadcast_to(array[None], (count, *array.shape)), axis, 0, 0, tiled=True
    )


def collect(array, axis, dim):
    return in_order(copy_for_each(array, axis), dim)


def tally_bins(stacked, levels):
    series, day_count, cell_count = stacked.shape
    day_block = math.gcd(day_count, max(1, 16384 // cell_count))

    def add_block(turn_index, totals):
        portion = lax.dynamic_slice_in_dim(stacked, turn_index * day_block, day_block, 1)
        matches = (portion[..., None] == levels).astype(jnp.bfloat16)
        return totals + jnp.sum(matches, axis=1, dtype=jnp.float32)

    initial = jnp.zeros((series, cell_count, levels.shape[0]), jnp.float32)
    return lax.fori_loop(0, day_count // day_block, add_block, initial)


def quantile_at(rank_rows, before_rows, pooled_rows):
    ramp_terms = jnp.minimum(
        jnp.maximum(rank_rows[:, :, None] - before_rows[:, None, :], 0.0), pooled_rows[:, None, :]
    )
    return jnp.sum(ramp_terms / jnp.maximum(pooled_rows, 1.0)[:, None, :], axis=2)


def build_table(totals, zone_rows, zone_share, widths, offsets, day_total):
    zone_terms = jnp.einsum(
        "cr,srb->scb",
        zone_rows,
        zone_share,
        precision=lax.Precision.HIGHEST,
        preferred_element_type=jnp.float32,
    )
    pooled = totals + pool_weight * day_total * zone_terms
    bins_total = pooled.shape[2]
    ladder = jnp.arange(bins_total, dtype=jnp.int32)
    upper_mask = (ladder[:, None] <= ladder[None, :]).astype(jnp.float32)
    running = jnp.einsum(
        "scb,bd->scd",
        pooled,
        upper_mask,
        precision=lax.Precision.HIGHEST,
        preferred_element_type=jnp.float32,
    )
    before = running - pooled
    future_rank = before[2] + 0.5 * pooled[2]
    row_count = pooled.shape[1]
    group_size = math.gcd(row_count, 128)
    group_count = row_count // group_size

    def per_group(group_rows):
        rank_rows, obs_before, obs_pooled, hist_before, hist_pooled = group_rows
        return (
            quantile_at(rank_rows, obs_before, obs_pooled),
            quantile_at(rank_rows, hist_before, hist_pooled),
        )

    shaped = (
        future_rank.reshape(group_count, group_size, bins_total),
        before[1].reshape(group_count, group_size, bins_total),
        pooled[1].reshape(group_count, group_size, bins_total),
        before[0].reshape(group_count, group_size, bins_total),
        pooled[0].reshape(group_count, group_size, bins_total),
    )
    quant_obs, quant_hist = lax.map(per_group, shaped)
    quant_obs = quant_obs.reshape(row_count, bins_total)
    quant_hist = quant_hist.reshape(row_count, bins_total)
    centers = (ladder.astype(jnp.float32) + 0.5)[None, :]
    return offsets[:, None] + widths[:, None] * (centers + quant_obs - quant_hist)


def apply_table(fut_bin, lookup, levels):
    day_count, cell_count = fut_bin.shape
    day_block = math.gcd(day_count, max(1, 16384 // cell_count))
    folded = fut_bin.reshape(day_count // day_block, day_block, cell_count)

    def select_rows(bins_rows):
        matches = bins_rows[..., None] == levels
        return jnp.sum(jnp.where(matches, lookup[None], 0.0), axis=2)

    return lax.map(select_rows, folded).reshape(day_count, cell_count)


def body(hist_bin, obs_bin, fut_bin, region_id, bin_width, bin_offset):
    day_count, cell_count = hist_bin.shape
    levels = jnp.arange(BINS, dtype=jnp.int32)
    stacked = jnp.stack([hist_bin, obs_bin, fut_bin])
    totals = tally_bins(stacked, levels)
    zone_rows = (region_id[:, None] == jnp.arange(REGIONS, dtype=jnp.int32)[None, :]).astype(
        jnp.float32
    )
    zone_part = jnp.einsum(
        "cr,scb->srb",
        zone_rows,
        totals,
        precision=lax.Precision.HIGHEST,
        preferred_element_type=jnp.float32,
    )
    zone_counts = lax.psum(zone_part, ("tm", "cells"))
    zone_share = zone_counts / jnp.sum(zone_counts, axis=2, keepdims=True)
    day_total = day_count * lax.axis_size("tm")
    share_rows = lax.psum_scatter(totals, "tm", scatter_dimension=1, tiled=True)
    share_count = share_rows.shape[1]
    first_row = lax.axis_index("tm") * share_count
    share_zones = lax.dynamic_slice_in_dim(zone_rows, first_row, share_count, 0)
    share_widths = lax.dynamic_slice_in_dim(bin_width, first_row, share_count, 0)
    share_offsets = lax.dynamic_slice_in_dim(bin_offset, first_row, share_count, 0)
    partial_table = build_table(
        share_rows, share_zones, zone_share, share_widths, share_offsets, day_total
    )
    lookup = collect(partial_table, "tm", 0)
    return apply_table(fut_bin, lookup, levels)


def solution(mesh):
    placed = (
        P("tm", "cells"),
        P("tm", "cells"),
        P("tm", "cells"),
        P("cells"),
        P("cells"),
        P("cells"),
    )
    return jax.shard_map(
        body, mesh=mesh, in_specs=placed, out_specs=P("tm", "cells"), check_vma=False
    )
```

profile of v0, /device:TPU:1, one launch (start us, length us, event | category | flops | bytes accessed | tf_op | source)
XLA Modules:
  0.0 995.9 jit_solution(16803068548199994457)
XLA Ops:
  7.4 6.6 pad_add_fusion
  14.0 453.7 %while.31 = (s32[]{:T(128)}, f32[3,1024,256]{2,1,0:T(8,128)}, s32[3,512,1024]{2,1,0:T(8,128)}, s32[]{:T(128)}, s32[]{:T(128)}, /*index=5*/s32[]{:T(128)}, s32[]{:T(128)}) while((s32[]{:T(128)}, f32[3,1024,256]{2,1,0:T(8,128)}, s32[3,512,1024]{2,1,0:T(8,128)}, s32[]{:T(128)}, s32[]{:T(128)}, /*index=5*/s32[]{:T(128)}, ...), condition=%wide.region_2.0_spmd.clone, body=%wide.region_0.0_spmd.clone.sunk | while | flops 51118084 | bytes 13172873 | solution.py:39
  15.0 9.3 convert_reduce_fusion.2
  27.3 9.3 convert_reduce_fusion.2
  41.6 9.3 convert_reduce_fusion.2
  55.8 9.3 convert_reduce_fusion.2
  70.0 9.3 convert_reduce_fusion.2
  84.3 9.3 convert_reduce_fusion.2
  98.5 9.3 convert_reduce_fusion.2
  112.7 9.3 convert_reduce_fusion.2
  127.0 9.3 convert_reduce_fusion.2
  141.2 9.3 convert_reduce_fusion.2
  155.5 9.3 convert_reduce_fusion.2
  169.7 9.3 convert_reduce_fusion.2
  183.9 9.3 convert_reduce_fusion.2
  198.2 9.3 convert_reduce_fusion.2
  212.4 9.3 convert_reduce_fusion.2
  226.6 9.3 convert_reduce_fusion.2
  240.9 9.3 convert_reduce_fusion.2
  255.1 9.3 convert_reduce_fusion.2
  269.4 9.3 convert_reduce_fusion.2
  283.6 9.3 convert_reduce_fusion.2
  297.8 9.3 convert_reduce_fusion.2
  312.1 9.3 convert_reduce_fusion.2
  326.3 9.3 convert_reduce_fusion.2
  340.5 9.3 convert_reduce_fusion.2
  354.8 9.3 convert_reduce_fusion.2
  369.0 9.3 convert_reduce_fusion.2
  383.2 9.3 convert_reduce_fusion.2
  397.5 9.3 convert_reduce_fusion.2
  411.7 9.3 convert_reduce_fusion.2
  426.0 9.3 convert_reduce_fusion.2
  440.2 9.3 convert_reduce_fusion.2
  454.4 9.3 convert_reduce_fusion.2
  467.7 5.4 convolution_bitcast_fusion
  475.5 253.2 %all-reduce.2.cloned.1.call-done = f32[3,128,256]{1,2,0:T(8,128)} async-done(((f32[3,128,256]{1,2,0:T(8,128)}), f32[3,128,256]{1,2,0:T(8,128)}) %all-reduce.2.cloned.1.call-update) | async-done | bytes 393232 | tf_op jit(solution)/shard_map/psum | solution.py:122
  736.6 6.3 all-to-all-start
  742.8 26.6 %all-to-all-done = f32[32,32,256]{2,1,0:T(8,128)S(1)} async-done(((f32[32,32,256]{2,1,0:T(8,128)}), f32[32,32,256]{2,1,0:T(8,128)S(1)}, u32[]{:S(2)}, u32[]{:S(2)}) %all-to-all-start) | async-done | bytes 1048608 | tf_op jit(solution)/shard_map/all_to_all | solution.py:20
  769.5 219.0 %while.30 = (s32[]{:T(128)}, f32[32,16,1024]{2,1,0:T(8,128)}, s32[32,16,1024]{2,1,0:T(8,128)}, f32[32,32,256]{2,1,0:T(8,128)S(1)}, s32[]{:T(128)}) while((s32[]{:T(128)}, f32[32,16,1024]{2,1,0:T(8,128)}, s32[32,16,1024]{2,1,0:T(8,128)}, f32[32,32,256]{2,1,0:T(8,128)S(1)}, s32[]{:T(128)}) %tuple.66), condition=%wide.region_10.11_spmd.clone, body=%wide.region_8.10_spmd.clone.sunk | while | flops 12566530 | bytes 1442369 | solution.py:104
  770.3 5.3 select_reduce_fusion.2
  777.2 5.3 select_reduce_fusion.2
  784.0 5.3 select_reduce_fusion.2
  790.8 5.3 select_reduce_fusion.2
  797.7 5.3 select_reduce_fusion.2
  804.5 5.3 select_reduce_fusion.2
  811.4 5.3 select_reduce_fusion.2
  818.2 5.3 select_reduce_fusion.2
  825.1 5.3 select_reduce_fusion.2
  831.9 5.3 select_reduce_fusion.2
  838.8 5.3 select_reduce_fusion.2
  845.6 5.3 select_reduce_fusion.2
  852.4 5.3 select_reduce_fusion.2
  859.3 5.3 select_reduce_fusion.2
  866.1 5.3 select_reduce_fusion.2
  873.0 5.3 select_reduce_fusion.2
  879.8 5.3 select_reduce_fusion.2
  886.7 5.3 select_reduce_fusion.2
  893.5 5.3 select_reduce_fusion.2
  900.3 5.3 select_reduce_fusion.2
  907.2 5.3 select_reduce_fusion.2
  914.0 5.3 select_reduce_fusion.2
  920.9 5.3 select_reduce_fusion.2
  927.7 5.3 select_reduce_fusion.2
  934.6 5.3 select_reduce_fusion.2
  (156 shorter events, 251.4 us)
Async XLA Ops:
  7.4 721.3 %all-reduce.2.cloned.1.call-start = ((), (), s32[]{:S(2)}) async-start(), calls=%async_computation.3 | async-start | bytes 786432 | tf_op jit(solution)/shard_map/psum | solution.py:122
  14.0 453.7 %copy-start = (s32[1024]{0:T(1024)S(1)}, s32[1024]{0:T(1024)}, u32[]{:S(2)}) copy-start(s32[1024]{0:T(1024)} %param.13) | copy-start | bytes 12292
  473.2 256.6 %reduce-scatter.2.cloned.1.call-start = ((), (), s32[]{:S(2)}) async-start(), calls=%async_computation.2 | async-start | bytes 3244032 | tf_op jit(solution)/shard_map/reduce_scatter | solution.py:125
  736.6 32.9 %all-to-all-start = ((f32[32,32,256]{2,1,0:T(8,128)}), f32[32,32,256]{2,1,0:T(8,128)S(1)}, u32[]{:S(2)}, u32[]{:S(2)}) async-start(f32[32,32,256]{2,1,0:T(8,128)} %broadcast_in_dim.68), calls=%async_computation.1 | async-start | bytes 2097152 | tf_op jit(solution)/shard_map/all_to_all | solution.py:20
Sparse Core Ops, SparseCore 0:
  473.3 255.3 all-reduce.1
Sparse Core Ops, SparseCore 1:
  476.2 149.1 reduce-scatter.1
where the time goes:
time: 1000 us; the launch traced here: 996 us
  other arithmetic  606 us (61%)
  waiting for transfers between devices  280 us (28%)
  local copies, waits for them, and re-layouts  80.2 us (8%)
  between operations  14.9 us (1%)
    reduce_sum x32, other arithmetic, add_block(): return totals + jnp.sum(matches, axis=1, dtype=jnp.float32)  297 us
    psum x1, waiting for transfers between devices, body(): zone_counts = lax.psum(zone_part, ('tm', 'cells'))  253 us
    reduce_sum x32, other arithmetic, select_rows(): return jnp.sum(jnp.where(matches, lookup[None], 0.0), axis=2)  171 us
    add x32, other arithmetic, add_block(): return totals + jnp.sum(matches, axis=1, dtype=jnp.float32)  126 us
    dynamic_slice x32, local copies, waits for them, and re-layouts, add_block(): lax.dynamic_slice_in_dim(stacked, turn_index * day_block, day_block, 1)  30.1 us
    eq x32, local copies, waits for them, and re-layouts, select_rows(): matches = bins_rows[..., None] == levels  27 us
    all_to_all x1, waiting for transfers between devices, copy_for_each(): lax.all_to_all(jnp.broadcast_to(array[None], (count, *array.shape)), axis...  26.6 us
    dynamic_update_slice x32, local copies, waits for them, and re-layouts, apply_table(): return lax.map(select_rows, folded).reshape(day_count, cell_count)  20.5 us
  transfers between devices with their start and end apart: 3, of which 2 were waited for; matrix products, arithmetic and copies ran while one was open for 0% of the time, Pallas kernels for 0%

commit v1 on v0

--- a/solution.py
+++ b/solution.py
@@ -119,7 +119,7 @@
         precision=lax.Precision.HIGHEST,
         preferred_element_type=jnp.float32,
     )
-    zone_counts = lax.psum(zone_part, ("tm", "cells"))
+    zone_counts = lax.psum(lax.psum(zone_part, "cells"), "tm")
     zone_share = zone_counts / jnp.sum(zone_counts, axis=2, keepdims=True)
     day_total = day_count * lax.axis_size("tm")
     share_rows = lax.psum_scatter(totals, "tm", scatter_dimension=1, tiled=True)

time: 1000 us -> 1280 us (1.28)
  waiting for transfers between devices: 280 us -> 549 us
    reduce_scatter x1, waiting for transfers between devices: 0.02 us -> 147 us  [body(): share_rows = lax.psum_scatter(totals, 'tm', scatter_dimension=1, tiled=True)]
    psum x1 -> x2, waiting for transfers between devices: 253 us -> 374 us  [body(): zone_counts = lax.psum(lax.psum(zone_part, 'cells'), 'tm')]
  transfers between devices with their start and end apart: 3 -> 4, of which waited for: 2 -> 4; matrix products, arithmetic and copies ran while one was open for 0% -> 0% of each run, Pallas kernels for 0% -> 0%
where the time goes in v1:
time: 1280 us; the launch traced here: 1270 us
  other arithmetic  613 us (48%)
  waiting for transfers between devices  549 us (43%)
  local copies, waits for them, and re-layouts  80.2 us (6%)
  between operations  13.2 us (1%)
    psum x2, waiting for transfers between devices, body(): zone_counts = lax.psum(lax.psum(zone_part, 'cells'), 'tm')  374 us
    reduce_sum x32, other arithmetic, add_block(): return totals + jnp.sum(matches, axis=1, dtype=jnp.float32)  297 us
    reduce_sum x32, other arithmetic, select_rows(): return jnp.sum(jnp.where(matches, lookup[None], 0.0), axis=2)  171 us
    reduce_scatter x1, waiting for transfers between devices, body(): share_rows = lax.psum_scatter(totals, 'tm', scatter_dimension=1, tiled=True)  147 us
    add x32, other arithmetic, add_block(): return totals + jnp.sum(matches, axis=1, dtype=jnp.float32)  133 us
    dynamic_slice x32, local copies, waits for them, and re-layouts, add_block(): lax.dynamic_slice_in_dim(stacked, turn_index * day_block, day_block, 1)  30.1 us
    eq x32, local copies, waits for them, and re-layouts, select_rows(): matches = bins_rows[..., None] == levels  27 us
    all_to_all x1, waiting for transfers between devices, copy_for_each(): lax.all_to_all(jnp.broadcast_to(array[None], (count, *array.shape)), axis...  26.8 us
  transfers between devices with their start and end apart: 4, of which 4 were waited for; matrix products, arithmetic and copies ran while one was open for 0% of the time, Pallas kernels for 0%

profile of v1, /device:TPU:1, one launch (start us, length us, event | category | flops | bytes accessed | tf_op | source)
XLA Modules:
  0.0 1272.8 jit_solution(1675923353319653063)
XLA Ops:
  6.5 6.6 pad_add_fusion
  13.2 460.2 %while.31 = (s32[]{:T(128)}, f32[3,1024,256]{2,1,0:T(8,128)}, s32[3,512,1024]{2,1,0:T(8,128)}, s32[]{:T(128)}, s32[]{:T(128)}, /*index=5*/s32[]{:T(128)}, s32[]{:T(128)}) while((s32[]{:T(128)}, f32[3,1024,256]{2,1,0:T(8,128)}, s32[3,512,1024]{2,1,0:T(8,128)}, s32[]{:T(128)}, s32[]{:T(128)}, /*index=5*/s32[]{:T(128)}, ...), condition=%wide.region_2.0_spmd.clone, body=%wide.region_0.0_spmd.clone.sunk | while | flops 51118084 | bytes 13172873 | solution.py:39
  14.1 9.3 convert_reduce_fusion.2
  26.7 9.3 convert_reduce_fusion.2
  41.1 9.3 convert_reduce_fusion.2
  55.6 9.3 convert_reduce_fusion.2
  70.0 9.3 convert_reduce_fusion.2
  84.4 9.3 convert_reduce_fusion.2
  98.9 9.3 convert_reduce_fusion.2
  113.3 9.3 convert_reduce_fusion.2
  127.8 9.3 convert_reduce_fusion.2
  142.2 9.3 convert_reduce_fusion.2
  156.6 9.3 convert_reduce_fusion.2
  171.1 9.3 convert_reduce_fusion.2
  185.5 9.3 convert_reduce_fusion.2
  200.0 9.3 convert_reduce_fusion.2
  214.4 9.3 convert_reduce_fusion.2
  228.8 9.3 convert_reduce_fusion.2
  243.3 9.3 convert_reduce_fusion.2
  257.7 9.3 convert_reduce_fusion.2
  272.1 9.3 convert_reduce_fusion.2
  286.6 9.3 convert_reduce_fusion.2
  301.0 9.3 convert_reduce_fusion.2
  315.5 9.3 convert_reduce_fusion.2
  329.9 9.3 convert_reduce_fusion.2
  344.3 9.3 convert_reduce_fusion.2
  358.8 9.3 convert_reduce_fusion.2
  373.2 9.3 convert_reduce_fusion.2
  387.7 9.3 convert_reduce_fusion.2
  402.1 9.3 convert_reduce_fusion.2
  416.5 9.3 convert_reduce_fusion.2
  431.0 9.3 convert_reduce_fusion.2
  445.4 9.3 convert_reduce_fusion.2
  459.8 9.3 convert_reduce_fusion.2
  473.3 5.4 convolution_bitcast_fusion
  478.8 107.6 %all-reduce.3.cloned.1.call-done = f32[3,128,256]{1,2,0:T(8,128)} async-done(((f32[3,128,256]{1,2,0:T(8,128)}), f32[3,128,256]{1,2,0:T(8,128)}) %all-reduce.3.cloned.1.call-update) | async-done | bytes 393232 | tf_op jit(solution)/shard_map/psum | solution.py:122
  588.9 266.9 %all-reduce.5.cloned.1.call-done = f32[3,128,256]{1,2,0:T(8,128)} async-done(((f32[3,128,256]{1,2,0:T(8,128)}), f32[3,128,256]{1,2,0:T(8,128)}) %all-reduce.5.cloned.1.call-update) | async-done | bytes 393232 | tf_op jit(solution)/shard_map/psum | solution.py:122
  856.9 147.4 %reduce-scatter.2.cloned.1.call-done = f32[3,32,256]{2,1,0:T(8,128)} async-done(((f32[3,1024,256]{2,1,0:T(8,128)}), f32[3,32,256]{2,1,0:T(8,128)}) %reduce-scatter.2.cloned.1.call-update) | async-done | bytes 98320 | tf_op jit(solution)/shard_map/reduce_scatter | solution.py:125
  1011.0 9.4 all-to-all-start
  1020.5 26.8 %all-to-all-done = f32[32,32,256]{2,1,0:T(8,128)S(1)} async-done(((f32[32,32,256]{2,1,0:T(8,128)}), f32[32,32,256]{2,1,0:T(8,128)S(1)}, u32[]{:S(2)}, u32[]{:S(2)}) %all-to-all-start) | async-done | bytes 1048608 | tf_op jit(solution)/shard_map/all_to_all | solution.py:20
  1047.2 219.0 %while.30 = (s32[]{:T(128)}, f32[32,16,1024]{2,1,0:T(8,128)}, s32[32,16,1024]{2,1,0:T(8,128)}, f32[32,32,256]{2,1,0:T(8,128)S(1)}, s32[]{:T(128)}) while((s32[]{:T(128)}, f32[32,16,1024]{2,1,0:T(8,128)}, s32[32,16,1024]{2,1,0:T(8,128)}, f32[32,32,256]{2,1,0:T(8,128)S(1)}, s32[]{:T(128)}) %tuple.68), condition=%wide.region_11.12_spmd.clone, body=%wide.region_9.11_spmd.clone.sunk | while | flops 12566530 | bytes 1442369 | solution.py:104
  1048.1 5.3 select_reduce_fusion.2
  1054.9 5.3 select_reduce_fusion.2
  1061.8 5.3 select_reduce_fusion.2
  1068.6 5.3 select_reduce_fusion.2
  1075.5 5.3 select_reduce_fusion.2
  1082.3 5.3 select_reduce_fusion.2
  1089.1 5.3 select_reduce_fusion.2
  1096.0 5.3 select_reduce_fusion.2
  1102.8 5.3 select_reduce_fusion.2
  1109.7 5.3 select_reduce_fusion.2
  1116.5 5.3 select_reduce_fusion.2
  1123.4 5.3 select_reduce_fusion.2
  1130.2 5.3 select_reduce_fusion.2
  1137.0 5.3 select_reduce_fusion.2
  1143.9 5.3 select_reduce_fusion.2
  1150.7 5.3 select_reduce_fusion.2
  1157.6 5.3 select_reduce_fusion.2
  1164.4 5.3 select_reduce_fusion.2
  1171.3 5.3 select_reduce_fusion.2
  1178.1 5.3 select_reduce_fusion.2
  1185.0 5.3 select_reduce_fusion.2
  1191.8 5.3 select_reduce_fusion.2
  1198.6 5.3 select_reduce_fusion.2
  (159 shorter events, 268.7 us)
Async XLA Ops:
  6.5 579.9 %all-reduce.3.cloned.1.call-start = ((), (), s32[]{:S(2)}) async-start(), calls=%async_computation.3 | async-start | bytes 786432 | tf_op jit(solution)/shard_map/psum | solution.py:122
  13.2 460.2 %copy-start = (s32[1024]{0:T(1024)S(1)}, s32[1024]{0:T(1024)}, u32[]{:S(2)}) copy-start(s32[1024]{0:T(1024)} %param.13) | copy-start | bytes 12292
  478.8 377.0 %all-reduce.5.cloned.1.call-start = ((), (), s32[]{:S(2)}) async-start(), calls=%async_computation.4 | async-start | bytes 786432 | tf_op jit(solution)/shard_map/psum | solution.py:122
  586.4 417.8 %reduce-scatter.2.cloned.1.call-start = ((), (), s32[]{:S(2)}) async-start(), calls=%async_computation.2 | async-start | bytes 3244032 | tf_op jit(solution)/shard_map/reduce_scatter | solution.py:125
  1011.0 36.2 %all-to-all-start = ((f32[32,32,256]{2,1,0:T(8,128)}), f32[32,32,256]{2,1,0:T(8,128)S(1)}, u32[]{:S(2)}, u32[]{:S(2)}) async-start(f32[32,32,256]{2,1,0:T(8,128)} %broadcast_in_dim.68), calls=%async_computation.1 | async-start | bytes 2097152 | tf_op jit(solution)/shard_map/all_to_all | solution.py:20
Sparse Core Ops, SparseCore 0:
  478.9 107.4 all-reduce.2
  589.0 266.7 all-reduce.4
  858.3 145.8 reduce-scatter.1
